TPU v7x, 32 devices: a whole 2x2x4 slice. The times are simulated.
32 devices in a mesh: bas: 8 (over y, x, core), aux: 4 (over z).
Axes of the slice: x: 2, y: 2, z: 4, core: 2. Of those that a mesh axis runs over, the one named last changes fastest.
Arguments:
- integrals: bfloat16 [4, 8192, 8192], P('aux', 'bas'), may hold values from -6 to 6
- screen: int32 [4, 64, 64], P('aux', 'bas'), may hold values from 0 to 1, as said below
- coefficients: bfloat16 [8192, 384], P('bas'), may hold values from -0.0625 to 0.0625
- weights: float32 [384], replicated, may hold values from -2 to 2
Outputs:
- exchange: bfloat16 [8192, 8192], P('aux', 'bas')
Inputs may be any that keep to these rules, and one draw needn't show every extreme that they name: `screen`: every block with equal row and column block index is 1; the share of ones differs from row block to row block.
All inputs are finite; a program needn't handle non-finite values.
Results may differ from a plain program's by a relative error of at most 0.018.
Values may be sent and summed in bfloat16 or wider, within the bound.
A program may use at most 128 MiB of HBM per device.

v0:
```python
import math
import jax
import jax.numpy as jnp
from jax import lax
from jax.sharding import PartitionSpec as P

NOCC = 384
BLOCK = 128
AUX_DEV = 1


def spread_2(block, axis, owner):
    block = jnp.where(lax.axis_index(axis) == owner, block, jnp.zeros_like(block))
    return lax.psum(block, axis)


def shards(integrals, screen, coefficients, weights):
    aux_count = integrals.shape[0]
    row_count = integrals.shape[1]
    basis_count = integrals.shape[2]
    occ_count = coefficients.shape[1]
    row_blocks = row_count // BLOCK
    col_blocks = basis_count // BLOCK
    masks = screen.reshape(aux_count, row_blocks, 1, col_blocks, 1).astype(jnp.bfloat16)
    masked = integrals.reshape(aux_count, row_blocks, BLOCK, col_blocks, BLOCK) * masks
    flat = masked.reshape(aux_count * row_count, basis_count)
    summed_half = jnp.dot(
        flat,
        lax.all_gather(coefficients, "bas", axis=0, tiled=True),
        preferred_element_type=jnp.float32,
    )
    half = summed_half.reshape(aux_count, row_count, occ_count).transpose(1, 0, 2)
    half = half.reshape(row_count, aux_count * occ_count).astype(jnp.bfloat16)
    aux_groups = lax.axis_size("aux")
    scale = 1.0 / math.sqrt(AUX_DEV * aux_groups * NOCC)
    every = lax.all_gather(half, "aux", axis=1, tiled=True)
    weighted_all = (every.astype(jnp.float32) * jnp.tile(weights, aux_count * aux_groups)).astype(
        jnp.bfloat16
    )
    spread = lax.axis_size("bas") // aux_groups
    first = lax.axis_index("aux") * spread
    received = [spread_2(every, "bas", first + offset) for offset in range(spread)]
    owned = jnp.concatenate(received, axis=0)
    per_group = aux_count * occ_count
    left = owned.reshape(owned.shape[0], aux_groups, per_group)
    right = weighted_all.reshape(row_count, aux_groups, per_group)
    terms = jnp.einsum("ngk,mgk->gnm", left, right, preferred_element_type=jnp.float32)
    rounded = lax.optimization_barrier(terms.astype(jnp.bfloat16))
    total = jnp.sum(rounded.astype(jnp.float32), axis=0)
    return (total * scale).astype(jnp.bfloat16)


def solution(mesh):
    in_specs = (P("aux", "bas", None), P("aux", "bas", None), P("bas", None), P())
    out_specs = P("aux", "bas")
    return jax.shard_map(shards, mesh=mesh, in_specs=in_specs, out_specs=out_specs, check_vma=False)
```

profile of v0, /device:TPU:0, one launch (start us, length us, event | category | flops | bytes accessed | tf_op | source)
XLA Modules:
  0.0 303.1 jit_solution(3715893133542091083)
XLA Ops:
  6.5 0.0 all-gather.3.cloned.1.call-start
  6.5 0.7 all-gather.3.cloned.1.call-update
  7.3 0.0 all-gather.5.cloned.1.call-start
  7.3 0.7 convert_bitcast_fusion
  8.0 49.4 %all-gather.3.cloned.1.call-done = bf16[8192,384]{1,0:T(8,128)(2,1)} async-done(((bf16[1024,384]{1,0:T(8,128)(2,1)}), bf16[8192,384]{1,0:T(8,128)(2,1)}) %all-gather.3.cloned.1.call-update) | async-done | bytes 6291472 | tf_op jit(solution)/shard_map/all_gather | solution.py:29
  57.4 6.5 %mul.33 = bf16[8,128,64,128]{3,2,1,0:T(8,128)(2,1)} broadcast(bf16[8,64]{1,0:T(8,128)(2,1)S(1)} %convert_bitcast_fusion), dimensions={0,2} | broadcast | bytes 16778240 | tf_op jit(solution)/shard_map/mul | solution.py:25
  63.8 26.9 %fusion.7 = bf16[1024,384]{1,0:T(8,128)(2,1)} fusion(bf16[8192,384]{1,0:T(8,128)(2,1)} %all-gather.3.cloned.1.call-done, bf16[128,8,64,128]{3,2,1,0:T(8,128)(2,1)} %bitcast.25, bf16[1,1024,8192]{2,1,0:T(8,128)(2,1)} %param.4), kind=kOutput, calls=%fused_computation.15 | convolution fusion | flops 6451232768 | bytes 40632320 | tf_op jit(solution)/shard_map/dot_general | solution.py:27
  90.7 0.0 all-gather.5.cloned.1.call-update
  90.7 0.2 all-reduce.3.cloned.1.call-start
  90.9 0.0 copy-start.2
  91.0 63.1 %all-gather.5.cloned.1.call-done = bf16[1024,1536]{1,0:T(8,128)(2,1)} async-done(((bf16[1024,384]{1,0:T(8,128)(2,1)}), bf16[1024,1536]{1,0:T(8,128)(2,1)}) %all-gather.5.cloned.1.call-update) | async-done | bytes 3145744 | tf_op jit(solution)/shard_map/all_gather | solution.py:36
  154.1 0.0 copy-start
  154.1 5.2 %broadcast_select_fusion.1 = (bf16[1024,1536]{1,0:T(8,128)(2,1)}, bf16[1024,1536]{1,0:T(8,128)(2,1)}) fusion(bf16[1024,1536]{1,0:T(8,128)(2,1)} %all-gather.5.cloned.1.call-done, pred[]{:T(512)S(6)} %eq.6, pred[]{:T(512)S(6)} %eq.7), kind=kLoop, calls=%fused_computation.14 | loop fusion | flops 3145728 | bytes 9437186 | tf_op jit(solution)/shard_map/jit(_where)/select_n | solution.py:13
  159.3 0.0 all-reduce.3.cloned.1.call-update
  159.3 0.0 copy-done.2
  159.3 0.0 copy-done
  159.3 2.3 multiply_convert_fusion.1
  161.6 100.4 %all-reduce.3.cloned.1.call-done = (bf16[1024,1536]{1,0:T(8,128)(2,1)}, bf16[1024,1536]{1,0:T(8,128)(2,1)}) async-done(((bf16[1024,1536]{1,0:T(8,128)(2,1)}, bf16[1024,1536]{1,0:T(8,128)(2,1)}), (bf16[1024,1536]{1,0:T(8,128)(2,1)}, bf16[1024,1536]{1,0:T(8,128)(2,1)})) %all-reduce.3.cloned.1.call-update) | async-done | bytes 6291472 | tf_op jit(solution)/shard_map/psum | solution.py:14
  262.0 0.0 copy-start.1
  262.0 6.1 %pad_maximum_fusion = bf16[2048,1536]{1,0:T(8,128)(2,1)} fusion(bf16[1024,1536]{1,0:T(8,128)(2,1)} %get-tuple-element.5, bf16[1024,1536]{1,0:T(8,128)(2,1)} %get-tuple-element.6), kind=kLoop, calls=%fused_computation.9 | loop fusion | flops 12582912 | bytes 12582912 | tf_op jit(solution)/shard_map/concatenate | solution.py:43
  268.0 0.0 copy-done.1
  268.0 15.3 %convolution_convert_fusion = bf16[4,2048,1024]{2,1,0:T(8,128)(2,1)} fusion(bf16[256,4,8,384]{3,2,1,0:T(8,128)(2,1)} %bitcast.26, bf16[128,4,8,384]{3,2,1,0:T(8,128)(2,1)S(1)} %bitcast.27), kind=kOutput, calls=%fused_computation.5 | convolution fusion | flops 6450839552 | bytes 26214400 | tf_op jit(solution)/shard_map/ngk,mgk->gnm/dot_general | solution.py:47
  283.3 9.8 %convert_reduce_fusion = f32[2048,1024]{1,0:T(8,128)S(1)} fusion(bf16[4,2048,1024]{2,1,0:T(8,128)(2,1)} %convolution_convert_fusion), kind=kLoop, calls=%fused_computation | loop fusion | flops 14680064 | bytes 25165824 | tf_op jit(solution)/shard_map/reduce_sum | solution.py:49
  293.2 3.4 %multiply_convert_fusion = bf16[2048,1024]{1,0:T(8,128)(2,1)} fusion(f32[2048,1024]{1,0:T(8,128)S(1)} %convert_reduce_fusion), kind=kLoop, calls=%fused_computation.6 | loop fusion | flops 4194304 | bytes 12582912 | tf_op jit(solution)/shard_map/convert_element_type | solution.py:50
  (2 shorter events, 0.0 us)
Async XLA Ops:
  6.5 50.8 %all-gather.3.cloned.1.call-start = ((), (), s32[]{:S(2)}) async-start(), calls=%async_computation | async-start | bytes 7077888 | tf_op jit(solution)/shard_map/all_gather | solution.py:29
  7.3 146.8 %all-gather.5.cloned.1.call-start = ((), (), s32[]{:S(2)}) async-start(), calls=%async_computation.1 | async-start | bytes 3932160 | tf_op jit(solution)/shard_map/all_gather | solution.py:36
  90.7 171.3 %all-reduce.3.cloned.1.call-start = ((), (), s32[]{:S(2)}) async-start(), calls=%async_computation.2 | async-start | bytes 12582912 | tf_op jit(solution)/shard_map/psum | solution.py:14
  90.9 68.3 %copy-start.2 = (f32[384]{0:T(512)S(1)}, f32[384]{0:T(512)}, u32[]{:S(2)}) copy-start(f32[384]{0:T(512)} %param.7) | copy-start | bytes 4612
  154.1 5.2 %copy-start = (bf16[1024,1536]{1,0:T(8,128)(2,1)S(1)}, bf16[1024,1536]{1,0:T(8,128)(2,1)}, u32[]{:S(2)}) copy-start(bf16[1024,1536]{1,0:T(8,128)(2,1)} %all-gather.5.cloned.1.call-done) | copy-start | bytes 9437188
  262.0 6.1 %copy-start.1 = (bf16[1024,1536]{1,0:T(8,128)(2,1)S(1)}, bf16[1024,1536]{1,0:T(8,128)(2,1)}, u32[]{:S(2)}) copy-start(bf16[1024,1536]{1,0:T(8,128)(2,1)} %multiply_convert_fusion.1) | copy-start | bytes 9437188
Sparse Core Ops, SparseCore 0:
  9.2 48.1 all-gather.2
  90.8 63.2 all-gather.4
  159.4 102.5 all-reduce.2
where the time goes:
time: 303 us
  waiting for transfers between devices  214 us (71%)
  matrix products  42.1 us (14%)
  other arithmetic  27.4 us (9%)
  between operations  13.2 us (4%)
  local copies, waits for them, and re-layouts  6.49 us (2%)
    psum x1, waiting for transfers between devices, spread_2(): return lax.psum(block, axis)  100 us
    all_gather x1, waiting for transfers between devices, shards(): every = lax.all_gather(half, 'aux', axis=1, tiled=True)  63.1 us
    all_gather x1, waiting for transfers between devices, shards(): lax.all_gather(coefficients, 'bas', axis=0, tiled=True)  49.4 us
    dot_general x1, matrix products, shards(): jnp.dot(flat, lax.all_gather(coefficients, 'bas', axis=0, tiled=True), pr...  26.9 us
    dot_general x1, matrix products, shards(): jnp.einsum('ngk,mgk->gnm', left, right, preferred_element_type=jnp.float32)  15.3 us
    reduce_sum x1, other arithmetic, shards(): total = jnp.sum(rounded.astype(jnp.float32), axis=0)  9.83 us
    mul x1, local copies, waits for them, and re-layouts, shards(): integrals.reshape(aux_count, row_blocks, BLOCK, col_blocks, BLOCK) * masks  6.46 us
  transfers between devices with their start and end apart: 3, of which 3 were waited for; matrix products, arithmetic and copies ran while one was open for 1% of the time, Pallas kernels for 0%

commit v1 on v0

--- a/solution.py
+++ b/solution.py
@@ -11,7 +11,11 @@
 
 def spread_2(block, axis, owner):
     block = jnp.where(lax.axis_index(axis) == owner, block, jnp.zeros_like(block))
-    return lax.psum(block, axis)
+
+    def raise_windows_here(shard_in):
+        return jnp.sum(lax.all_gather(shard_in, axis_name=axis), axis=0)
+
+    return raise_windows_here(block)
 
 
 def shards(integrals, screen, coefficients, weights):

time: 303 us -> 476 us (1.57)
  waiting for transfers between devices: 214 us -> 347 us
  other arithmetic: 27.4 us -> 56.6 us
  local copies, waits for them, and re-layouts: 6.49 us -> 15.3 us
    all_gather x0 -> x2, waiting for transfers between devices: none -> 233 us  [raise_windows_here(): return jnp.sum(lax.all_gather(shard_in, axis_name=axis), axis=0)]
    psum x1 -> x0, waiting for transfers between devices: 100 us -> none  [spread_2(): return lax.psum(block, axis)]
    reduce_sum x0 -> x2, other arithmetic: none -> 30.4 us  [raise_windows_here(): return jnp.sum(lax.all_gather(shard_in, axis_name=axis), axis=0)]
    concatenate x0 -> x1, local copies, waits for them, and re-layouts: none -> 8.76 us  [shards(): owned = jnp.concatenate(received, axis=0)]
  transfers between devices with their start and end apart: 3 -> 4, of which waited for: 3 -> 4; matrix products, arithmetic and copies ran while one was open for 1% -> 4% of each run, Pallas kernels for 0% -> 0%
where the time goes in v1:
time: 476 us; the launch traced here: 475 us
  waiting for transfers between devices  347 us (73%)
  other arithmetic  56.6 us (12%)
  matrix products  43.1 us (9%)
  local copies, waits for them, and re-layouts  15.3 us (3%)
  between operations  13.2 us (3%)
    all_gather x2, waiting for transfers between devices, raise_windows_here(): return jnp.sum(lax.all_gather(shard_in, axis_name=axis), axis=0)  233 us
    all_gather x1, waiting for transfers between devices, shards(): every = lax.all_gather(half, 'aux', axis=1, tiled=True)  63.3 us
    all_gather x1, waiting for transfers between devices, shards(): lax.all_gather(coefficients, 'bas', axis=0, tiled=True)  49.4 us
    reduce_sum x2, other arithmetic, raise_windows_here(): return jnp.sum(lax.all_gather(shard_in, axis_name=axis), axis=0)  30.4 us
    dot_general x1, matrix products, shards(): jnp.dot(flat, lax.all_gather(coefficients, 'bas', axis=0, tiled=True), pr...  26.8 us
    dot_general x1, matrix products, shards(): jnp.einsum('ngk,mgk->gnm', left, right, preferred_element_type=jnp.float32)  16.2 us
    reduce_sum x1, other arithmetic, shards(): total = jnp.sum(rounded.astype(jnp.float32), axis=0)  9.83 us
  transfers between devices with their start and end apart: 4, of which 4 were waited for; matrix products, arithmetic and copies ran while one was open for 4% of the time, Pallas kernels for 0%

profile of v1, /device:TPU:0, one launch (start us, length us, event | category | flops | bytes accessed | tf_op | source)
XLA Modules:
  0.0 475.3 jit_solution(13883535933825530539)
XLA Ops:
  6.5 0.0 all-gather.7.cloned.1.call-start
  6.5 0.7 all-gather.7.cloned.1.call-update
  7.3 0.0 all-gather.9.cloned.1.call-start
  7.3 0.7 convert_bitcast_fusion
  8.0 49.4 %all-gather.7.cloned.1.call-done = bf16[8192,384]{1,0:T(8,128)(2,1)} async-done(((bf16[1024,384]{1,0:T(8,128)(2,1)}), bf16[8192,384]{1,0:T(8,128)(2,1)}) %all-gather.7.cloned.1.call-update) | async-done | bytes 6291472 | tf_op jit(solution)/shard_map/all_gather | solution.py:33
  57.4 6.5 %mul.33 = bf16[8,128,64,128]{3,2,1,0:T(8,128)(2,1)} broadcast(bf16[8,64]{1,0:T(8,128)(2,1)S(1)} %convert_bitcast_fusion), dimensions={0,2} | broadcast | bytes 16778240 | tf_op jit(solution)/shard_map/mul | solution.py:29
  63.8 26.8 %fusion.5 = bf16[1024,384]{1,0:T(8,128)(2,1)} fusion(bf16[8192,384]{1,0:T(8,128)(2,1)} %all-gather.7.cloned.1.call-done, bf16[128,8,64,128]{3,2,1,0:T(8,128)(2,1)} %bitcast.27, bf16[1,1024,8192]{2,1,0:T(8,128)(2,1)} %param.4), kind=kOutput, calls=%fused_computation.13 | convolution fusion | flops 6451232768 | bytes 40632320 | tf_op jit(solution)/shard_map/dot_general | solution.py:31
  90.7 0.0 all-gather.9.cloned.1.call-update
  90.7 0.0 all-gather.11.cloned.1.call-start
  90.8 0.0 copy-start.2
  90.8 63.3 %all-gather.9.cloned.1.call-done = bf16[1024,1536]{1,0:T(8,128)(2,1)} async-done(((bf16[1024,384]{1,0:T(8,128)(2,1)}), bf16[1024,1536]{1,0:T(8,128)(2,1)}) %all-gather.9.cloned.1.call-update) | async-done | bytes 3145744 | tf_op jit(solution)/shard_map/all_gather | solution.py:40
  154.1 0.0 copy-start
  154.1 5.1 %broadcast_select_fusion.1 = (bf16[1024,1536]{1,0:T(8,128)(2,1)}, bf16[1024,1536]{1,0:T(8,128)(2,1)}) fusion(bf16[1024,1536]{1,0:T(8,128)(2,1)} %all-gather.9.cloned.1.call-done, pred[]{:T(512)S(6)} %eq.6, pred[]{:T(512)S(6)} %eq.7), kind=kLoop, calls=%fused_computation.12 | loop fusion | flops 3145728 | bytes 9437186 | tf_op jit(solution)/shard_map/jit(_where)/select_n | solution.py:13
  159.2 0.0 all-gather.11.cloned.1.call-update
  159.2 0.2 all-gather.13.cloned.1.call-start
  159.4 0.3 all-gather.13.cloned.1.call-update
  159.8 0.0 copy-done.2
  159.8 0.0 copy-done
  159.8 2.2 multiply_convert_fusion.1
  162.1 121.1 %all-gather.11.cloned.1.call-done = bf16[8192,1536]{1,0:T(8,128)(2,1)} async-done(((bf16[1024,1536]{1,0:T(8,128)(2,1)}), bf16[8192,1536]{1,0:T(8,128)(2,1)}) %all-gather.11.cloned.1.call-update) | async-done | bytes 25165840 | tf_op jit(solution)/shard_map/all_gather | solution.py:16
  283.2 14.9 %reduce_sum.33 = bf16[1024,1536]{1,0:T(8,128)(2,1)S(1)} reduce(bf16[8,1024,1536]{2,1,0:T(8,128)(2,1)} %bitcast.25, bf16[]{:T(256)} %constant.17.clone.1), dimensions={0}, to_apply=%region_0.1 | reduce | flops 11010048 | bytes 28311554 | tf_op jit(solution)/shard_map/reduce_sum | solution.py:16
  298.1 112.0 %all-gather.13.cloned.1.call-done = bf16[8192,1536]{1,0:T(8,128)(2,1)} async-done(((bf16[1024,1536]{1,0:T(8,128)(2,1)}), bf16[8192,1536]{1,0:T(8,128)(2,1)}) %all-gather.13.cloned.1.call-update) | async-done | bytes 25165840 | tf_op jit(solution)/shard_map/all_gather | solution.py:16
  410.1 15.5 %reduce_sum.34 = bf16[1024,1536]{1,0:T(8,128)(2,1)} reduce(bf16[8,1024,1536]{2,1,0:T(8,128)(2,1)} %bitcast.26, bf16[]{:T(256)} %constant.17.clone.1), dimensions={0}, to_apply=%region_1.2 | reduce | flops 11010048 | bytes 28311554 | tf_op jit(solution)/shard_map/reduce_sum | solution.py:16
  425.6 5.0 %pad_maximum_fusion = bf16[2048,1536]{1,0:T(8,128)(2,1)} fusion(bf16[1024,1536]{1,0:T(8,128)(2,1)} %reduce_sum.34, bf16[1024,1536]{1,0:T(8,128)(2,1)S(1)} %reduce_sum.33), kind=kLoop, calls=%fused_computation.7 | loop fusion | flops 12582912 | bytes 12582912 | tf_op jit(solution)/shard_map/concatenate | solution.py:47
  430.5 0.0 copy-start.1
  430.5 8.8 %copy.8 = bf16[2048,1536]{0,1:T(8,128)(2,1)} copy(bf16[2048,1536]{1,0:T(8,128)(2,1)} %pad_maximum_fusion) | data formatting | bytes 12582912 | tf_op jit(solution)/shard_map/concatenate | solution.py:47
  439.3 0.0 copy-done.1
  439.3 16.2 %convolution_convert_fusion = bf16[4,2048,1024]{2,1,0:T(8,128)(2,1)} fusion(bf16[2048,4,384]{0,2,1:T(8,128)(2,1)} %bitcast.28, bf16[128,4,8,384]{3,2,1,0:T(8,128)(2,1)S(1)} %bitcast.29), kind=kOutput, calls=%fused_computation.5 | convolution fusion | flops 6450839552 | bytes 26214400 | tf_op jit(solution)/shard_map/ngk,mgk->gnm/dot_general | solution.py:51
  455.5 9.8 %convert_reduce_fusion = f32[2048,1024]{1,0:T(8,128)S(1)} fusion(bf16[4,2048,1024]{2,1,0:T(8,128)(2,1)} %convolution_convert_fusion), kind=kLoop, calls=%fused_computation | loop fusion | flops 14680064 | bytes 25165824 | tf_op jit(solution)/shard_map/reduce_sum | solution.py:53
  465.4 3.4 multiply_convert_fusion
  (2 shorter events, 0.0 us)
Async XLA Ops:
  6.5 50.8 %all-gather.7.cloned.1.call-start = ((), (), s32[]{:S(2)}) async-start(), calls=%async_computation | async-start | bytes 7077888 | tf_op jit(solution)/shard_map/all_gather | solution.py:33
  7.3 146.8 %all-gather.9.cloned.1.call-start = ((), (), s32[]{:S(2)}) async-start(), calls=%async_computation.1 | async-start | bytes 3932160 | tf_op jit(solution)/shard_map/all_gather | solution.py:40
  90.7 192.5 %all-gather.11.cloned.1.call-start = ((), (), s32[]{:S(2)}) async-start(), calls=%async_computation.2 | async-start | bytes 28311552 | tf_op jit(solution)/shard_map/all_gather | solution.py:16
  90.8 69.0 %copy-start.2 = (f32[384]{0:T(512)S(1)}, f32[384]{0:T(512)}, u32[]{:S(2)}) copy-start(f32[384]{0:T(512)} %param.7) | copy-start | bytes 4612
  154.1 5.7 %copy-start = (bf16[1024,1536]{1,0:T(8,128)(2,1)S(1)}, bf16[1024,1536]{1,0:T(8,128)(2,1)}, u32[]{:S(2)}) copy-start(bf16[1024,1536]{1,0:T(8,128)(2,1)} %all-gather.9.cloned.1.call-done) | copy-start | bytes 9437188
  159.2 250.9 %all-gather.13.cloned.1.call-start = ((), (), s32[]{:S(2)}) async-start(), calls=%async_computation.3 | async-start | bytes 28311552 | tf_op jit(solution)/shard_map/all_gather | solution.py:16
  430.5 8.8 %copy-start.1 = (bf16[1024,1536]{1,0:T(8,128)(2,1)S(1)}, bf16[1024,1536]{1,0:T(8,128)(2,1)}, u32[]{:S(2)}) copy-start(bf16[1024,1536]{1,0:T(8,128)(2,1)} %multiply_convert_fusion.1) | copy-start | bytes 9437188
Sparse Core Ops, SparseCore 0:
  9.2 48.1 all-gather.6
  90.8 63.2 all-gather.8
  159.3 123.7 all-gather.10
  284.9 125.1 all-gather.12
